TPU v7x, 128 devices: a whole 4x4x4 slice. The times are simulated.
128 devices in a mesh: grp: 4 (over z_lo, core), dev: 32 (over y, z_hi, x).
Axes of the slice: x: 4, y: 4, z: 4 (z_hi: 2, z_lo: 2; z = z_hi * 2 + z_lo), core: 2. Of those that a mesh axis runs over, the one named last changes fastest.
Arguments:
- tokens: bfloat16 [16384, 2048], P(('grp', 'dev')), may hold values from -6 to 6
- queries: bfloat16 [16384, 2048], P(('grp', 'dev')), may hold values from -7.5 to 7.5
- suffix_keys: bfloat16 [16384, 2048], P(('grp', 'dev')), may hold values from -6 to 6
- suffix_values: bfloat16 [16384, 2048], P(('grp', 'dev')), may hold values from -6 to 6
- prefix_keys: bfloat16 [4, 1024, 2048], P('grp', 'dev'), may hold values from -6 to 6
- prefix_values: bfloat16 [4, 1024, 2048], P('grp', 'dev'), may hold values from -6 to 6
- out_weight: bfloat16 [2048, 2048], replicated, may hold values from -0.125 to 0.125
- norm_gain: float32 [2048], replicated, may hold values from 0.1 to 1.9
- routes: int32 [16384, 6], P(('grp', 'dev')), may hold values from 0 to 63, all different within a row; in each aligned block of 128 rows (0 to 127, 128 to 255, ...) at most 16 rows name the same one
- route_weights: float32 [16384, 6], P(('grp', 'dev')), may hold values from 0.05 to 0.5
- gate_up_weight: bfloat16 [128, 2048, 1408], P(('grp', 'dev')), may hold values from -0.125 to 0.125
- down_weight: bfloat16 [128, 704, 2048], P(('grp', 'dev')), may hold values from -0.15625 to 0.15625
Outputs:
- attended: bfloat16 [16384, 2048], P(('grp', 'dev'))
- routed: bfloat16 [16384, 2048], P(('grp', 'dev'))
Inputs may be any that keep to these rules, and one draw needn't show every extreme that they name: `routes`: each row names 6 different experts. Within the rows of one request (aligned blocks of 128 rows) no expert is named by more than 16 rows, and in some block one expert is named exactly 16 times.
All inputs are finite; a program needn't handle non-finite values.
Results may differ from a plain program's by a relative error of at most 0.019.
Values may be sent and summed in bfloat16 or wider, within the bound.
A program may use at most 128 MiB of HBM per device.

v0:
```python
import math
import jax
import jax.numpy as jnp
from jax import lax
from jax.sharding import PartitionSpec as P

HEADS = 16
HEAD_DIM = 128
TOP = 6


def half_expert(rows, gate_up, down_proj):
    hidden_units = down_proj.shape[0]
    projected = jnp.dot(rows, gate_up, preferred_element_type=jnp.float32)
    active = (jax.nn.silu(projected[:, :hidden_units]) * projected[:, hidden_units:]).astype(
        jnp.bfloat16
    )
    return jnp.dot(active, down_proj, preferred_element_type=jnp.float32).astype(jnp.bfloat16)


def on_device(
    tokens,
    queries,
    suffix_keys,
    suffix_values,
    prefix_keys,
    prefix_values,
    out_weight,
    norm_gain,
    routes,
    route_weights,
    gate_up_weight,
    down_weight,
):
    rows_here = tokens.shape[0]
    width = tokens.shape[1]
    divisor = math.sqrt(HEAD_DIM)
    query_heads = queries.reshape(rows_here, HEADS, HEAD_DIM)
    running_max = jnp.full((HEADS, rows_here), -jnp.inf, jnp.float32)
    denominator = jnp.zeros((HEADS, rows_here), jnp.float32)
    weighted = jnp.zeros((HEADS, rows_here, HEAD_DIM), jnp.float32)
    key_piece = lax.all_gather(prefix_keys[0], "dev", axis=0, tiled=True).reshape(
        -1, HEADS, HEAD_DIM
    )
    value_piece = lax.all_gather(prefix_values[0], "dev", axis=0, tiled=True).reshape(
        -1, HEADS, HEAD_DIM
    )
    scores = (
        jnp.einsum("rhd,khd->hrk", query_heads, key_piece, preferred_element_type=jnp.float32)
        / divisor
    )
    new_max = jnp.max(scores, axis=-1)
    shifted = jnp.exp(scores - new_max[..., None])
    factor = jnp.exp(running_max - new_max)
    denominator = denominator * factor + jnp.sum(shifted, axis=-1)
    weighted = weighted * factor[..., None] + jnp.einsum(
        "hrk,khd->hrd",
        shifted.astype(jnp.bfloat16),
        value_piece,
        preferred_element_type=jnp.float32,
    )
    causal = jnp.arange(rows_here)[:, None] >= jnp.arange(rows_here)[None, :]
    suffix_scores = (
        jnp.einsum(
            "rhd,khd->hrk",
            query_heads,
            suffix_keys.reshape(rows_here, HEADS, HEAD_DIM),
            preferred_element_type=jnp.float32,
        )
        / divisor
    )
    suffix_scores = jnp.where(causal[None], suffix_scores, -jnp.inf)
    suffix_max = jnp.max(suffix_scores, axis=-1)
    suffix_exp = jnp.exp(suffix_scores - suffix_max[..., None])
    suffix_sum = jnp.sum(suffix_exp, axis=-1)
    suffix_acc = jnp.einsum(
        "hrk,khd->hrd",
        suffix_exp.astype(jnp.bfloat16),
        suffix_values.reshape(rows_here, HEADS, HEAD_DIM),
        preferred_element_type=jnp.float32,
    )
    merged_max = jnp.maximum(new_max, suffix_max)
    prefix_scale = jnp.exp(new_max - merged_max)
    suffix_scale = jnp.exp(suffix_max - merged_max)
    mixed = (weighted * prefix_scale[..., None] + suffix_acc * suffix_scale[..., None]) / (
        denominator * prefix_scale + suffix_sum * suffix_scale
    )[..., None]
    heads_out = jnp.transpose(mixed, (1, 0, 2)).reshape(rows_here, width).astype(jnp.bfloat16)
    attended = jnp.dot(heads_out, out_weight, preferred_element_type=jnp.float32).astype(
        jnp.bfloat16
    )
    residual = tokens.astype(jnp.float32) + attended.astype(jnp.float32)
    mean_square = jnp.mean(residual * residual, axis=-1, keepdims=True)
    normed = (residual * lax.rsqrt(mean_square + 1e-06) * norm_gain).astype(jnp.bfloat16)
    groups = lax.axis_size("grp")
    members = lax.axis_size("dev")
    experts = groups * members // 2
    capacity = 4 * rows_here * TOP // (3 * experts)
    flat_routes = routes.reshape(-1)
    onehot = (flat_routes[:, None] == jnp.arange(experts, dtype=jnp.int32)[None, :]).astype(
        jnp.int32
    )
    ranking = jnp.sum(jnp.cumsum(onehot, axis=0) * onehot, axis=1) - 1
    slots = flat_routes * capacity + ranking
    owners = jnp.arange(rows_here * TOP, dtype=jnp.int32) // TOP
    outgoing = jnp.zeros((experts * capacity, width), jnp.bfloat16).at[slots].set(normed[owners])
    buffer = jnp.broadcast_to(
        outgoing.reshape(experts, 1, capacity, width), (experts, 2, capacity, width)
    ).reshape(2 * experts, capacity, width)
    received = lax.all_to_all(buffer, ("grp", "dev"), split_axis=0, concat_axis=0, tiled=True)
    partial_rows = half_expert(
        received.reshape(-1, width), gate_up_weight[0], down_weight[0]
    ).reshape(2 * experts, capacity, width)
    returned = lax.all_to_all(partial_rows, ("grp", "dev"), split_axis=0, concat_axis=0, tiled=True)
    halves = returned.reshape(experts, 2, capacity, width)
    expert_table = lax.optimization_barrier(
        (halves[:, 0].astype(jnp.float32) + halves[:, 1].astype(jnp.float32)).astype(jnp.bfloat16)
    ).reshape(experts * capacity, width)
    picked = expert_table[slots].astype(jnp.float32)
    weighted_rows = picked * route_weights.reshape(-1)[:, None]
    routed = jnp.sum(weighted_rows.reshape(rows_here, TOP, width), axis=1).astype(jnp.bfloat16)
    return (attended, routed)


def solution(mesh):
    return jax.shard_map(
        on_device,
        mesh=mesh,
        in_specs=(
            P(("grp", "dev"), None),
            P(("grp", "dev"), None),
            P(("grp", "dev"), None),
            P(("grp", "dev"), None),
            P("grp", "dev", None),
            P("grp", "dev", None),
            P(),
            P(),
            P(("grp", "dev"), None),
            P(("grp", "dev"), None),
            P(("grp", "dev"), None, None),
            P(("grp", "dev"), None, None),
        ),
        out_specs=(P(("grp", "dev"), None), P(("grp", "dev"), None)),
        check_vma=False,
    )
```

profile of v0, /device:TPU:1, one launch (start us, length us, event | category | flops | bytes accessed | tf_op | source)
XLA Modules:
  0.0 513.5 jit_solution(7477060815687853919)
XLA Ops:
  7.2 0.0 copy-start
  7.2 0.0 all-gather.5.cloned.1.call-start
  7.2 0.7 all-gather.5.cloned.1.call-update
  7.9 0.0 all-gather.7.cloned.1.call-start
  8.0 0.7 all-gather.7.cloned.1.call-update
  8.7 0.8 copy.47
  9.5 0.1 eq.29
  9.6 0.1 eq.25
  9.7 2.0 copy.55
  11.8 1.8 reduce-window.6
  13.6 0.3 slice_reduce_fusion
  13.9 0.7 broadcast_multiply_fusion
  14.6 0.1 copy.46
  14.7 0.1 mul.102
  14.9 0.1 fusion.42
  15.1 0.0 copy-start.6
  15.1 1.8 fusion.56
  16.9 0.0 copy-start.4
  16.9 1.0 copy-done.4
  17.9 0.2 fusion.30
  18.0 77.1 %all-gather.5.cloned.1.call-done = bf16[1,1024,2048]{2,1,0:T(8,128)(2,1)} async-done(((bf16[1,32,2048]{2,1,0:T(8,128)(2,1)}), bf16[1,1024,2048]{2,1,0:T(8,128)(2,1)}) %all-gather.5.cloned.1.call-update) | async-done | bytes 4194320 | tf_op jit(solution)/shard_map/all_gather | solution.py:42
  95.2 6.4 %copy.38 = bf16[1,1024,2048]{1,2,0:T(8,128)(2,1)} copy(bf16[1,1024,2048]{2,1,0:T(8,128)(2,1)} %all-gather.5.cloned.1.call-done) | data formatting | bytes 8388608 | tf_op jit(solution)/shard_map/all_gather | solution.py:42
  101.6 0.0 copy-done.6
  101.6 3.5 multiply_reduce_fusion.1
  105.1 0.0 copy-start.1
  105.1 3.2 copy-done.1
  108.3 1.8 fusion
  110.1 67.4 %all-gather.7.cloned.1.call-done = bf16[1,1024,2048]{2,1,0:T(8,128)(2,1)} async-done(((bf16[1,32,2048]{2,1,0:T(8,128)(2,1)}), bf16[1,1024,2048]{2,1,0:T(8,128)(2,1)}) %all-gather.7.cloned.1.call-update) | async-done | bytes 4194320 | tf_op jit(solution)/shard_map/all_gather | solution.py:45
  177.5 6.4 %copy.41 = bf16[1,1024,2048]{1,2,0:T(8,128)(2,1)} copy(bf16[1,1024,2048]{2,1,0:T(8,128)(2,1)} %all-gather.7.cloned.1.call-done) | data formatting | bytes 8388608 | tf_op jit(solution)/shard_map/all_gather | solution.py:45
  183.9 0.0 slice-start
  183.9 0.0 copy-start.5
  183.9 0.0 copy-start.7
  183.9 0.0 slice-start.1
  183.9 0.0 copy-start.2
  184.0 6.9 %fusion.26 = f32[128,16,128]{0,2,1:T(8,128)S(1)} fusion(bf16[1024,16,128]{0,2,1:T(8,128)(2,1)} %bitcast.121, f32[16,128,1024]{2,1,0:T(8,128)} %copy-done.1, f32[16,128]{1,0:T(8,128)S(1)} %get-tuple-element.6, f32[128,16]{0,1:T(8,128)S(1)} %get-tuple-element.4, f32[128,16]{0,1:T(8,128)S(1)} %get-tuple-element.5), kind=kOutput, calls=%fused_computation.34 | convolution fusion | flops 543686656 | bytes 13656064 | tf_op jit(solution)/shard_map/hrk,khd->hrd/dot_general | solution.py:56
  190.9 0.0 copy-done.5
  190.9 0.0 copy-done.7
  190.9 0.3 fusion.29
  191.2 0.0 slice-done
  191.3 0.3 slice-done.1
  191.6 0.0 copy-done.2
  191.6 0.0 copy-start.8
  191.6 1.4 multiply_reduce_fusion.2
  193.0 0.0 copy-start.3
  193.0 0.8 copy-done.3
  193.8 0.0 copy-done.8
  193.8 0.2 multiply_convert_fusion
  194.0 23.5 %scatter_custom_fusion = bf16[1024,2048]{1,0:T(8,128)(2,1)} fusion(s32[768]{0:T(1024)S(1)} %fusion.50, bf16[128,2048]{1,0:T(8,128)(2,1)S(1)} %multiply_convert_fusion, s32[1024]{0:T(1024)S(1)} %pad_clamp_fusion.1, bf16[]{:T(256)} %constant.17.clone.1), kind=kCustom, calls=%fused_computation.20 | custom fusion | bytes 4194306 | tf_op jit(solution)/shard_map/scatter | solution.py:106
  217.5 6.8 %broadcast_in_dim.28 = bf16[64,2,16,2048]{3,2,1,0:T(8,128)(2,1)} broadcast(bf16[64,16,2048]{2,1,0:T(8,128)(2,1)} %bitcast.120), dimensions={0,2,3} | broadcast | bytes 12582912 | tf_op jit(solution)/shard_map/broadcast_in_dim | solution.py:107
  224.3 105.2 %all_to_all.10 = bf16[128,16,2048]{2,1,0:T(8,128)(2,1)S(1)} all-to-all(bf16[128,16,2048]{2,1,0:T(8,128)(2,1)} %bitcast.117), channel_id=1, replica_groups=mesh['grp'=4,'dev'=32] {'grp','dev'}, dimensions={0} | all-to-all | bytes 16777216 | tf_op jit(solution)/shard_map/all_to_all | solution.py:110
  329.5 17.8 %fusion.3 = f32[2048,1408]{0,1:T(8,128)} fusion(bf16[2048,2048]{1,0:T(8,128)(2,1)S(1)} %bitcast.124, bf16[1,2048,1408]{2,1,0:T(8,128)(2,1)} %param.22), kind=kOutput, calls=%fused_computation.12 | convolution fusion | flops 11811160064 | bytes 25690112 | tf_op jit(solution)/shard_map/dot_general | solution.py:14
  347.3 0.0 copy-done
  347.3 13.5 %convolution_convert_fusion = bf16[2048,2048]{1,0:T(8,128)(2,1)} fusion(f32[2048,1408]{0,1:T(8,128)} %fusion.3, bf16[1,704,2048]{2,1,0:T(8,128)(2,1)S(1)} %copy-done), kind=kOutput, calls=%fused_computation.7 | convolution fusion | flops 5918425088 | bytes 22806528 | tf_op jit(solution)/shard_map/dot_general | solution.py:18
  360.8 0.0 copy-start.9
  360.8 7.9 %all-to-all-start.1 = ((bf16[128,16,2048]{2,1,0:T(8,128)(2,1)}), bf16[128,16,2048]{2,1,0:T(8,128)(2,1)}, u32[]{:S(2)}, u32[]{:S(2)}) async-start(bf16[128,16,2048]{2,1,0:T(8,128)(2,1)} %bitcast.123), calls=%async_computation.1 | async-start | bytes 16777216 | tf_op jit(solution)/shard_map/all_to_all | solution.py:114
  368.7 0.0 copy-done.9
  368.7 0.1 copy.52
  368.8 108.1 %all-to-all-done.1 = bf16[128,16,2048]{2,1,0:T(8,128)(2,1)} async-done(((bf16[128,16,2048]{2,1,0:T(8,128)(2,1)}), bf16[128,16,2048]{2,1,0:T(8,128)(2,1)}, u32[]{:S(2)}, u32[]{:S(2)}) %all-to-all-start.1) | async-done | bytes 8388640 | tf_op jit(solution)/shard_map/all_to_all | solution.py:114
  477.0 5.7 %fusion.7 = bf16[64,16,2048]{2,1,0:T(8,128)(2,1)} fusion(bf16[64,2,16,2048]{3,2,1,0:T(8,128)(2,1)} %bitcast.17), kind=kLoop, calls=%fused_computation.15 | loop fusion | flops 8388608 | bytes 12582912 | tf_op jit(solution)/shard_map/convert_element_type | solution.py:117
  482.7 9.8 %gather_fusion = bf16[768,2048]{1,0:T(8,128)(2,1)} fusion(bf16[1024,2048]{1,0:T(8,128)(2,1)} %bitcast.116, s32[1024]{0:T(1024)S(1)} %pad_clamp_fusion), kind=kCustom, calls=%fused_computation.1 | custom fusion | bytes 6294528 | tf_op jit(solution)/shard_map/gather | solution.py:119
  492.5 6.6 %reshape.210 = f32[128,6,2048]{2,1,0:T(8,128)} reshape(bf16[768,2048]{1,0:T(8,128)(2,1)} %gather_fusion) | data formatting | bytes 9437184 | tf_op jit(solution)/shard_map/convert_element_type | solution.py:119
  499.1 7.4 %multiply_reduce_fusion = bf16[128,2048]{1,0:T(8,128)(2,1)} fusion(f32[128,6,2048]{2,1,0:T(8,128)} %reshape.210, f32[128,6]{1,0:T(8,128)S(1)} %copy.52), kind=kLoop, calls=%fused_computation.3 | loop fusion | flops 2883584 | bytes 6818816 | tf_op jit(solution)/shard_map/reduce_sum | solution.py:121
  (11 shorter events, 0.1 us)
Async XLA Ops:
  7.2 340.1 %copy-start = (bf16[1,704,2048]{2,1,0:T(8,128)(2,1)S(1)}, bf16[1,704,2048]{2,1,0:T(8,128)(2,1)}, u32[]{:S(2)}) copy-start(bf16[1,704,2048]{2,1,0:T(8,128)(2,1)} %param.23) | copy-start | bytes 8650756
  7.2 88.0 %all-gather.5.cloned.1.call-start = ((), (), s32[]{:S(2)}) async-start(), calls=%async_computation.2 | async-start | bytes 4325376 | tf_op jit(solution)/shard_map/all_gather | solution.py:42
  7.9 169.6 %all-gather.7.cloned.1.call-start = ((), (), s32[]{:S(2)}) async-start(), calls=%async_computation.3 | async-start | bytes 4325376 | tf_op jit(solution)/shard_map/all_gather | solution.py:45
  15.1 86.5 %copy-start.6 = (bf16[128,2048]{1,0:T(8,128)(2,1)S(1)}, bf16[128,2048]{1,0:T(8,128)(2,1)}, u32[]{:S(2)}) copy-start(bf16[128,2048]{1,0:T(8,128)(2,1)} %param.13) | copy-start | bytes 1572868
  16.9 1.0 copy-start.4
  105.1 3.2 copy-start.1
  183.9 7.3 %slice-start = ((s8[8388608]{0:T(1024)(128)(4,1)}), s8[4194304]{0:T(1024)(128)(4,1)S(1)}, s32[]{:S(2)}) async-start(s8[8388608]{0:T(1024)(128)(4,1)} %bitcast.118), calls=%async_computation.4 | async-start | bytes 8388608
  183.9 7.0 %copy-start.5 = (f32[16,128,128]{1,2,0:T(8,128)S(1)}, f32[16,128,128]{1,2,0:T(8,128)}, u32[]{:S(2)}) copy-start(f32[16,128,128]{1,2,0:T(8,128)} %copy-done.4) | copy-start | bytes 3145732
  183.9 7.0 %copy-start.7 = (bf16[128,2048]{0,1:T(8,128)(2,1)S(1)}, bf16[128,2048]{0,1:T(8,128)(2,1)}, u32[]{:S(2)}) copy-start(bf16[128,2048]{0,1:T(8,128)(2,1)} %copy.55) | copy-start | bytes 1572868
  183.9 7.7 %slice-start.1 = ((s8[8388608]{0:T(1024)(128)(4,1)}), s8[4194304]{0:T(1024)(128)(4,1)S(1)}, s32[]{:S(2)}) async-start(s8[8388608]{0:T(1024)(128)(4,1)} %bitcast.118), calls=%async_computation.5 | async-start | bytes 8388608
  183.9 7.6 %copy-start.2 = (bf16[128,2048]{1,0:T(8,128)(2,1)S(1)}, bf16[128,2048]{1,0:T(8,128)(2,1)}, u32[]{:S(2)}) copy-start(bf16[128,2048]{1,0:T(8,128)(2,1)} %param.12) | copy-start | bytes 1572868
  191.6 2.2 copy-start.8
  193.0 0.8 copy-start.3
  360.8 7.9 %copy-start.9 = (f32[128,6]{0,1:T(8,128)S(1)}, f32[128,6]{0,1:T(8,128)}, u32[]{:S(2)}) copy-start(f32[128,6]{0,1:T(8,128)} %param.21) | copy-start | bytes 9220
  360.8 116.2 %all-to-all-start.1 = ((bf16[128,16,2048]{2,1,0:T(8,128)(2,1)}), bf16[128,16,2048]{2,1,0:T(8,128)(2,1)}, u32[]{:S(2)}, u32[]{:S(2)}) async-start(bf16[128,16,2048]{2,1,0:T(8,128)(2,1)} %bitcast.123), calls=%async_computation.1 | async-start | bytes 16777216 | tf_op jit(solution)/shard_map/all_to_all | solution.py:114
Sparse Core Ops, SparseCore 0:
  11.0 84.1 all-gather.4
  98.2 79.3 all-gather.6
where the time goes:
time: 521 us; the launch traced here: 514 us
  waiting for transfers between devices  254 us (49%)
  blocking collectives  105 us (20%)
  local copies, waits for them, and re-layouts  68.5 us (13%)
  matrix products  45.2 us (9%)
  other arithmetic  18 us (3%)
  between operations  14.5 us (3%)
  starting transfers between devices  7.99 us (2%)
    all_to_all x1, waiting for transfers between devices, on_device(): lax.all_to_all(partial_rows, ('grp', 'dev'), split_axis=0, concat_axis=0,...  108 us
    all_to_all x1, blocking collectives, on_device(): lax.all_to_all(buffer, ('grp', 'dev'), split_axis=0, concat_axis=0, tiled...  105 us
    all_gather x1, waiting for transfers between devices, on_device(): lax.all_gather(prefix_keys[0], 'dev', axis=0, tiled=True)  77.1 us
    all_gather x1, waiting for transfers between devices, on_device(): lax.all_gather(prefix_values[0], 'dev', axis=0, tiled=True)  67.4 us
    scatter x1, local copies, waits for them, and re-layouts, on_device(): jnp.zeros((experts * capacity, width), jnp.bfloat16).at[slots]  23.5 us
    dot_general x1, matrix products, half_expert(): projected = jnp.dot(rows, gate_up, preferred_element_type=jnp.float32)  17.8 us
    dot_general x1, matrix products, half_expert(): jnp.dot(active, down_proj, preferred_element_type=jnp.float32)  13.5 us
  transfers between devices with their start and end apart: 3, of which 3 were waited for; matrix products, arithmetic and copies ran while one was open for 4% of the time, Pallas kernels for 0%

commit v1 on v0

--- a/solution.py
+++ b/solution.py
@@ -7,6 +7,14 @@
 HEADS = 16
 HEAD_DIM = 128
 TOP = 6
+
+
+def local_data_advance(work_x):
+    top = jnp.concatenate(
+        jax.lax.all_to_all(jnp.stack([work_x] * jax.lax.psum(1, "dev"), axis=0), "dev", 0, 0),
+        axis=0,
+    )
+    return top
 
 
 def half_expert(rows, gate_up, down_proj):
@@ -42,9 +50,7 @@
     key_piece = lax.all_gather(prefix_keys[0], "dev", axis=0, tiled=True).reshape(
         -1, HEADS, HEAD_DIM
     )
-    value_piece = lax.all_gather(prefix_values[0], "dev", axis=0, tiled=True).reshape(
-        -1, HEADS, HEAD_DIM
-    )
+    value_piece = local_data_advance(prefix_values[0]).reshape(-1, HEADS, HEAD_DIM)
     scores = (
         jnp.einsum("rhd,khd->hrk", query_heads, key_piece, preferred_element_type=jnp.float32)
         / divisor

time: 521 us -> 497 us (0.954)
  waiting for transfers between devices: 254 us -> 210 us
  starting transfers between devices: 7.99 us -> 19.7 us
    all_gather x1 -> x0, waiting for transfers between devices: 67.4 us -> none  [on_device(): lax.all_gather(prefix_values[0], 'dev', axis=0, tiled=True)]
    all_to_all x0 -> x1, waiting for transfers between devices: none -> 45.6 us  [local_data_advance(): jax.lax.all_to_all(jnp.stack([work_x] * jax.lax.psum(1, 'dev'), axis=0),...]
    all_gather x1, waiting for transfers between devices: 77.1 us -> 55.7 us  [on_device(): lax.all_gather(prefix_keys[0], 'dev', axis=0, tiled=True)]
    all_to_all x0 -> x1, starting transfers between devices: none -> 11.3 us  [local_data_advance(): jax.lax.all_to_all(jnp.stack([work_x] * jax.lax.psum(1, 'dev'), axis=0),...]
    scatter x1, local copies, waits for them, and re-layouts: 23.5 us -> 30.9 us  [on_device(): jnp.zeros((experts * capacity, width), jnp.bfloat16).at[slots]]
    all_gather x1 -> x0, local copies, waits for them, and re-layouts: 6.41 us -> none  [on_device(): lax.all_gather(prefix_values[0], 'dev', axis=0, tiled=True)]
  transfers between devices with their start and end apart: 3 -> 3, of which waited for: 3 -> 3; matrix products, arithmetic and copies ran while one was open for 4% -> 3% of each run, Pallas kernels for 0% -> 0%
where the time goes in v1:
time: 497 us; the launch traced here: 489 us
  waiting for transfers between devices  210 us (42%)
  blocking collectives  105 us (21%)
  local copies, waits for them, and re-layouts  73.7 us (15%)
  matrix products  47.8 us (10%)
  starting transfers between devices  19.7 us (4%)
  other arithmetic  18.2 us (4%)
  between operations  14.5 us (3%)
    all_to_all x1, waiting for transfers between devices, on_device(): lax.all_to_all(partial_rows, ('grp', 'dev'), split_axis=0, concat_axis=0,...  108 us
    all_to_all x1, blocking collectives, on_device(): lax.all_to_all(buffer, ('grp', 'dev'), split_axis=0, concat_axis=0, tiled...  105 us
    all_gather x1, waiting for transfers between devices, on_device(): lax.all_gather(prefix_keys[0], 'dev', axis=0, tiled=True)  55.7 us
    all_to_all x1, waiting for transfers between devices, local_data_advance(): jax.lax.all_to_all(jnp.stack([work_x] * jax.lax.psum(1, 'dev'), axis=0),...  45.6 us
    scatter x1, local copies, waits for them, and re-layouts, on_device(): jnp.zeros((experts * capacity, width), jnp.bfloat16).at[slots]  30.9 us
    dot_general x1, matrix products, half_expert(): projected = jnp.dot(rows, gate_up, preferred_element_type=jnp.float32)  17.8 us
    dot_general x1, matrix products, half_expert(): jnp.dot(active, down_proj, preferred_element_type=jnp.float32)  13.5 us
    all_to_all x1, starting transfers between devices, local_data_advance(): jax.lax.all_to_all(jnp.stack([work_x] * jax.lax.psum(1, 'dev'), axis=0),...  11.3 us
  transfers between devices with their start and end apart: 3, of which 3 were waited for; matrix products, arithmetic and copies ran while one was open for 3% of the time, Pallas kernels for 0%

profile of v1, /device:TPU:1, one launch (start us, length us, event | category | flops | bytes accessed | tf_op | source)
XLA Modules:
  0.0 488.9 jit_solution(12124428347087472853)
XLA Ops:
  7.2 0.0 copy-start
  7.2 0.0 all-gather.3.cloned.1.call-start
  7.2 0.7 all-gather.3.cloned.1.call-update
  7.9 0.0 copy-start.7
  7.9 0.0 copy-start.6
  7.9 3.5 stack.3
  11.4 11.3 %all-to-all-start = ((bf16[32,32,2048]{2,1,0:T(8,128)(2,1)}), bf16[32,32,2048]{2,1,0:T(8,128)(2,1)}, u32[]{:S(2)}, u32[]{:S(2)}) async-start(bf16[32,32,2048]{2,1,0:T(8,128)(2,1)} %stack.3), calls=%async_computation | async-start | bytes 8388608 | tf_op jit(solution)/shard_map/all_to_all | solution.py:14
  22.8 0.0 copy-done.7
  22.8 0.1 copy.47
  22.9 0.1 eq.29
  23.0 0.1 eq.25
  23.2 0.0 copy-done.6
  23.2 1.0 copy.55
  24.2 1.8 reduce-window.6
  26.0 0.3 slice_reduce_fusion
  26.3 0.1 copy.46
  26.4 0.1 mul.102
  26.6 0.1 fusion.49
  26.8 1.7 fusion.63
  28.5 0.0 copy-start.4
  28.5 1.0 copy-done.4
  29.6 0.2 fusion.37
  29.7 45.6 %all-to-all-done = bf16[32,32,2048]{2,1,0:T(8,128)(2,1)} async-done(((bf16[32,32,2048]{2,1,0:T(8,128)(2,1)}), bf16[32,32,2048]{2,1,0:T(8,128)(2,1)}, u32[]{:S(2)}, u32[]{:S(2)}) %all-to-all-start) | async-done | bytes 4194336 | tf_op jit(solution)/shard_map/all_to_all | solution.py:14
  75.4 5.6 %copy.61 = bf16[128,8,16,128]{3,2,1,0:T(8,128)(2,1)} copy(bf16[128,8,16,128]{3,1,2,0:T(8,128)(2,1)} %bitcast.29) | data formatting | bytes 8388608
  80.9 0.0 copy-start.5
  80.9 55.7 %all-gather.3.cloned.1.call-done = bf16[1,1024,2048]{2,1,0:T(8,128)(2,1)} async-done(((bf16[1,32,2048]{2,1,0:T(8,128)(2,1)}), bf16[1,1024,2048]{2,1,0:T(8,128)(2,1)}) %all-gather.3.cloned.1.call-update) | async-done | bytes 4194320 | tf_op jit(solution)/shard_map/all_gather | solution.py:50
  136.6 6.4 %copy.38 = bf16[1,1024,2048]{1,2,0:T(8,128)(2,1)} copy(bf16[1,1024,2048]{2,1,0:T(8,128)(2,1)} %all-gather.3.cloned.1.call-done) | data formatting | bytes 8388608 | tf_op jit(solution)/shard_map/all_gather | solution.py:50
  143.0 0.0 copy-done.5
  143.0 3.5 multiply_reduce_fusion.1
  146.5 0.0 copy-start.1
  146.5 1.9 fusion
  148.4 0.3 copy-done.1
  148.7 0.0 copy-start.2
  148.7 4.4 fusion.31
  153.1 2.0 fusion.36
  155.2 0.0 copy-done.2
  155.2 0.0 copy-start.8
  155.2 4.8 multiply_reduce_fusion.2
  160.0 0.0 copy-start.3
  160.0 0.8 copy-done.3
  160.8 0.0 copy-done.8
  160.8 1.0 multiply_convert_fusion
  161.8 30.9 %scatter_custom_fusion = bf16[1024,2048]{1,0:T(8,128)(2,1)} fusion(s32[768]{0:T(1024)S(1)} %fusion.57, bf16[128,2048]{1,0:T(8,128)(2,1)} %multiply_convert_fusion, s32[1024]{0:T(1024)S(1)} %pad_clamp_fusion.1, bf16[]{:T(256)} %constant.17.clone.1), kind=kCustom, calls=%fused_computation.21 | custom fusion | bytes 4194816 | tf_op jit(solution)/shard_map/scatter | solution.py:112
  192.7 6.8 %broadcast_in_dim.28 = bf16[64,2,16,2048]{3,2,1,0:T(8,128)(2,1)} broadcast(bf16[64,16,2048]{2,1,0:T(8,128)(2,1)} %bitcast.120), dimensions={0,2,3} | broadcast | bytes 12582912 | tf_op jit(solution)/shard_map/broadcast_in_dim | solution.py:113
  199.5 105.0 %all_to_all.15 = bf16[128,16,2048]{2,1,0:T(8,128)(2,1)S(1)} all-to-all(bf16[128,16,2048]{2,1,0:T(8,128)(2,1)} %bitcast.119), channel_id=1, replica_groups=mesh['grp'=4,'dev'=32] {'grp','dev'}, dimensions={0} | all-to-all | bytes 16777216 | tf_op jit(solution)/shard_map/all_to_all | solution.py:116
  304.4 17.8 %fusion.3 = f32[2048,1408]{0,1:T(8,128)} fusion(bf16[2048,2048]{1,0:T(8,128)(2,1)S(1)} %bitcast.123, bf16[1,2048,1408]{2,1,0:T(8,128)(2,1)} %param.22), kind=kOutput, calls=%fused_computation.12 | convolution fusion | flops 11811160064 | bytes 25690112 | tf_op jit(solution)/shard_map/dot_general | solution.py:22
  322.2 0.0 copy-done
  322.2 13.5 %convolution_convert_fusion = bf16[2048,2048]{1,0:T(8,128)(2,1)} fusion(f32[2048,1408]{0,1:T(8,128)} %fusion.3, bf16[1,704,2048]{2,1,0:T(8,128)(2,1)S(1)} %copy-done), kind=kOutput, calls=%fused_computation.7 | convolution fusion | flops 5918425088 | bytes 22806528 | tf_op jit(solution)/shard_map/dot_general | solution.py:26
  335.8 0.0 copy-start.9
  335.8 8.3 %all-to-all-start.2 = ((bf16[128,16,2048]{2,1,0:T(8,128)(2,1)}), bf16[128,16,2048]{2,1,0:T(8,128)(2,1)}, u32[]{:S(2)}, u32[]{:S(2)}) async-start(bf16[128,16,2048]{2,1,0:T(8,128)(2,1)} %bitcast.122), calls=%async_computation.2 | async-start | bytes 16777216 | tf_op jit(solution)/shard_map/all_to_all | solution.py:120
  344.1 0.0 copy-done.9
  344.1 0.1 copy.52
  344.2 108.1 %all-to-all-done.2 = bf16[128,16,2048]{2,1,0:T(8,128)(2,1)} async-done(((bf16[128,16,2048]{2,1,0:T(8,128)(2,1)}), bf16[128,16,2048]{2,1,0:T(8,128)(2,1)}, u32[]{:S(2)}, u32[]{:S(2)}) %all-to-all-start.2) | async-done | bytes 8388640 | tf_op jit(solution)/shard_map/all_to_all | solution.py:120
  452.4 5.7 %fusion.7 = bf16[64,16,2048]{2,1,0:T(8,128)(2,1)} fusion(bf16[64,2,16,2048]{3,2,1,0:T(8,128)(2,1)} %bitcast.17), kind=kLoop, calls=%fused_computation.15 | loop fusion | flops 8388608 | bytes 12582912 | tf_op jit(solution)/shard_map/convert_element_type | solution.py:123
  458.1 9.8 %gather_fusion = bf16[768,2048]{1,0:T(8,128)(2,1)} fusion(bf16[1024,2048]{1,0:T(8,128)(2,1)} %bitcast.118, s32[1024]{0:T(1024)S(1)} %pad_clamp_fusion), kind=kCustom, calls=%fused_computation.1 | custom fusion | bytes 6294528 | tf_op jit(solution)/shard_map/gather | solution.py:125
  467.9 6.6 %reshape.207 = f32[128,6,2048]{2,1,0:T(8,128)} reshape(bf16[768,2048]{1,0:T(8,128)(2,1)} %gather_fusion) | data formatting | bytes 9437184 | tf_op jit(solution)/shard_map/convert_element_type | solution.py:125
  474.4 7.4 %multiply_reduce_fusion = bf16[128,2048]{1,0:T(8,128)(2,1)} fusion(f32[128,6,2048]{2,1,0:T(8,128)} %reshape.207, f32[128,6]{1,0:T(8,128)S(1)} %copy.52), kind=kLoop, calls=%fused_computation.3 | loop fusion | flops 2883584 | bytes 6818816 | tf_op jit(solution)/shard_map/reduce_sum | solution.py:127
  (11 shorter events, 0.1 us)
Async XLA Ops:
  7.2 315.1 %copy-start = (bf16[1,704,2048]{2,1,0:T(8,128)(2,1)S(1)}, bf16[1,704,2048]{2,1,0:T(8,128)(2,1)}, u32[]{:S(2)}) copy-start(bf16[1,704,2048]{2,1,0:T(8,128)(2,1)} %param.23) | copy-start | bytes 8650756
  7.2 129.4 %all-gather.3.cloned.1.call-start = ((), (), s32[]{:S(2)}) async-start(), calls=%async_computation.3 | async-start | bytes 4325376 | tf_op jit(solution)/shard_map/all_gather | solution.py:50
  7.9 14.8 %copy-start.7 = (s32[128,6]{0,1:T(8,128)S(1)}, s32[128,6]{0,1:T(8,128)}, u32[]{:S(2)}) copy-start(s32[128,6]{0,1:T(8,128)} %param.20) | copy-start | bytes 9220
  7.9 15.2 %copy-start.6 = (bf16[128,2048]{1,0:T(8,128)(2,1)S(1)}, bf16[128,2048]{1,0:T(8,128)(2,1)}, u32[]{:S(2)}) copy-start(bf16[128,2048]{1,0:T(8,128)(2,1)} %param.15) | copy-start | bytes 1572868
  11.4 63.9 %all-to-all-start = ((bf16[32,32,2048]{2,1,0:T(8,128)(2,1)}), bf16[32,32,2048]{2,1,0:T(8,128)(2,1)}, u32[]{:S(2)}, u32[]{:S(2)}) async-start(bf16[32,32,2048]{2,1,0:T(8,128)(2,1)} %stack.3), calls=%async_computation | async-start | bytes 8388608 | tf_op jit(solution)/shard_map/all_to_all | solution.py:14
  28.5 1.1 copy-start.4
  80.9 62.1 %copy-start.5 = (bf16[128,2048]{1,0:T(8,128)(2,1)S(1)}, bf16[128,2048]{1,0:T(8,128)(2,1)}, u32[]{:S(2)}) copy-start(bf16[128,2048]{1,0:T(8,128)(2,1)} %param.13) | copy-start | bytes 1572868
  146.5 2.2 copy-start.1
  148.7 6.5 %copy-start.2 = (bf16[128,2048]{1,0:T(8,128)(2,1)S(1)}, bf16[128,2048]{1,0:T(8,128)(2,1)}, u32[]{:S(2)}) copy-start(bf16[128,2048]{1,0:T(8,128)(2,1)} %param.12) | copy-start | bytes 1572868
  155.2 5.6 %copy-start.8 = (f32[2048]{0:T(1024)S(1)}, f32[2048]{0:T(1024)}, u32[]{:S(2)}) copy-start(f32[2048]{0:T(1024)} %param.19) | copy-start | bytes 24580
  160.0 0.8 copy-start.3
  335.8 8.3 %copy-start.9 = (f32[128,6]{0,1:T(8,128)S(1)}, f32[128,6]{0,1:T(8,128)}, u32[]{:S(2)}) copy-start(f32[128,6]{0,1:T(8,128)} %param.21) | copy-start | bytes 9220
  335.8 116.6 %all-to-all-start.2 = ((bf16[128,16,2048]{2,1,0:T(8,128)(2,1)}), bf16[128,16,2048]{2,1,0:T(8,128)(2,1)}, u32[]{:S(2)}, u32[]{:S(2)}) async-start(bf16[128,16,2048]{2,1,0:T(8,128)(2,1)} %bitcast.122), calls=%async_computation.2 | async-start | bytes 16777216 | tf_op jit(solution)/shard_map/all_to_all | solution.py:120
Sparse Core Ops, SparseCore 0:
  11.0 125.5 all-gather.2
